TPU v7x, 32 devices: a whole 2x2x4 slice. The times are simulated.
32 devices in a mesh: dp: 8 (over y, x, core), mp: 4 (over z).
Axes of the slice: x: 2, y: 2, z: 4, core: 2. Of those that a mesh axis runs over, the one named last changes fastest.
Arguments:
- act_in: bfloat16 [1024, 4096], P('dp', 'mp'), may hold values from -6 to 6
- grad_in: bfloat16 [1024, 16384], P('dp'), may hold values from -6 to 6
- query_act: bfloat16 [1024, 4096], P('dp', 'mp'), may hold values from -6 to 6
- query_grad: bfloat16 [1024, 16384], P('dp'), may hold values from -6 to 6
- act_basis: bfloat16 [4096, 128], P('mp'), may hold values from -1.1 to 1.1
- grad_basis: bfloat16 [16384, 128], P('dp'), may hold values from -1.1 to 1.1
- seq_lengths: int32 [4], replicated, may hold values from 1 to 256, 768 in all
Outputs:
- moments: float32 [4096, 16384], P('mp', 'dp')
- scores: float32 [64, 4], replicated
Inputs may be any that keep to these rules, and one draw needn't show every extreme that they name: `seq_lengths`: live tokens are the first ones of each sequence, and one sequence is full.
All inputs are finite; a program needn't handle non-finite values.
Results may differ from a plain program's by a relative error of at most 0.0046.
Values may be sent and summed in bfloat16 or wider, within the bound.
A program may use at most 192 MiB of HBM per device.

v0:
```python
import math
import jax
import jax.numpy as jnp
from jax import lax
from jax.sharding import PartitionSpec as P

D = 4096
FF = 16384
QUERIES = 64
QUERY_LEN = 16
damping = 0.1


def rotate(rows_in, basis_rows):
    count_rows, full_width = rows_in.shape
    block_size = basis_rows.shape[1]
    blocks = full_width // block_size
    product = jnp.einsum(
        "nbk,bkc->nbc",
        rows_in.reshape(count_rows, blocks, block_size),
        basis_rows.reshape(blocks, block_size, block_size),
        preferred_element_type=jnp.float32,
    )
    return product.reshape(count_rows, full_width)


def local(act_in, grad_in, query_act, query_grad, act_basis, grad_basis, seq_lengths):
    dp_count = lax.axis_size("dp")
    dp_index = lax.axis_index("dp")
    tok_dev = act_in.shape[0]
    seq_count = seq_lengths.shape[0]
    total_tokens = tok_dev * dp_count
    seq_len = total_tokens // seq_count
    global_rows = dp_index * tok_dev + jnp.arange(tok_dev, dtype=jnp.int32)
    seq_index = global_rows // seq_len
    within = global_rows % seq_len
    matches = seq_index[:, None] == jnp.arange(seq_count, dtype=jnp.int32)[None, :]
    row_length = jnp.sum(jnp.where(matches, seq_lengths[None, :], 0), axis=1)
    live_rows = (within < row_length).astype(jnp.float32)
    act_rot = (rotate(act_in, act_basis) * live_rows[:, None]).astype(jnp.bfloat16)
    query_act_rot = rotate(query_act, act_basis).astype(jnp.bfloat16)
    gathered_act, gathered_query = (
        lax.all_gather(act_rot, "dp", axis=0, tiled=True),
        lax.all_gather(query_act_rot, "dp", axis=0, tiled=True),
    )
    grad_cols, query_cols = (
        lax.all_to_all(grad_in, "dp", split_axis=1, concat_axis=0, tiled=True),
        lax.all_to_all(query_grad, "dp", split_axis=1, concat_axis=0, tiled=True),
    )
    grad_rot = rotate(grad_cols, grad_basis).astype(jnp.bfloat16)
    query_grad_rot = rotate(query_cols, grad_basis).astype(jnp.bfloat16)
    act_square = jnp.square(gathered_act.astype(jnp.float32)).astype(jnp.bfloat16)
    grad_square = jnp.square(grad_rot.astype(jnp.float32)).astype(jnp.bfloat16)
    counted = jnp.sum(seq_lengths).astype(jnp.float32)
    moments = (
        jnp.einsum("ti,tj->ij", act_square, grad_square, preferred_element_type=jnp.float32)
        / counted
    )
    weights = 1.0 / (moments + damping)
    act_width = gathered_act.shape[1]
    grad_width = grad_rot.shape[1]
    seq_acts = gathered_act.reshape(seq_count, seq_len, act_width)
    seq_grads = grad_rot.reshape(seq_count, seq_len, grad_width)
    seq_grad = jnp.einsum("sli,slj->sij", seq_acts, seq_grads, preferred_element_type=jnp.float32)
    scale_seq = lax.rsqrt(seq_lengths.astype(jnp.float32))
    precond = (weights[None, :, :] * seq_grad * scale_seq[:, None, None]).astype(jnp.bfloat16)
    mapped = jnp.einsum("ui,sij->suj", gathered_query, precond, preferred_element_type=jnp.float32)
    per_row = jnp.sum(mapped * query_grad_rot.astype(jnp.float32)[None, :, :], axis=2)
    per_query = jnp.sum(per_row.reshape(seq_count, QUERIES, QUERY_LEN), axis=2)
    partial_scores = per_query.T / math.sqrt(QUERY_LEN * D * FF)
    scores = lax.psum(partial_scores, ("dp", "mp"))
    return (moments, scores)


def solution(mesh):
    return jax.shard_map(
        local,
        mesh=mesh,
        in_specs=(
            P("dp", "mp"),
            P("dp", None),
            P("dp", "mp"),
            P("dp", None),
            P("mp", None),
            P("dp", None),
            P(),
        ),
        out_specs=(P("mp", "dp"), P()),
        check_vma=False,
    )
```

profile of v0, /device:TPU:0, one launch (start us, length us, event | category | flops | bytes accessed | tf_op | source)
XLA Modules:
  0.0 238.3 jit_solution(18068171213799246787)
XLA Ops:
  7.2 0.0 copy-start
  7.2 4.8 %copy.93 = bf16[16,8,8,2048]{3,2,0,1:T(8,128)(2,1)} copy(bf16[16,8,8,2048]{3,2,1,0:T(8,128)(2,1)} %bitcast.72) | data formatting | bytes 8388608 | tf_op jit(solution)/shard_map/all_to_all | solution.py:47
  12.0 5.3 %all-to-all-start = ((bf16[128,8,2048]{2,0,1:T(8,128)(2,1)}), bf16[128,8,2048]{2,0,1:T(8,128)(2,1)}, u32[]{:S(2)}, u32[]{:S(2)}) async-start(bf16[128,8,2048]{2,0,1:T(8,128)(2,1)} %bitcast.68), calls=%async_computation | async-start | bytes 8388608 | tf_op jit(solution)/shard_map/all_to_all | solution.py:47
  17.4 0.0 all-gather.3.cloned.1.call-start
  17.4 0.0 copy-done.2
  17.4 0.3 fusion.15
  17.8 0.2 copy.44
  18.0 0.1 select_reduce_fusion
  18.1 0.8 multiply_convert_fusion.4
  18.9 0.0 all-gather.3.cloned.1.call-update
  18.9 4.7 %copy.92 = bf16[16,8,8,2048]{3,2,0,1:T(8,128)(2,1)} copy(bf16[16,8,8,2048]{3,2,1,0:T(8,128)(2,1)} %bitcast.73) | data formatting | bytes 8388608 | tf_op jit(solution)/shard_map/all_to_all | solution.py:48
  23.7 51.3 %all-to-all-done = bf16[128,8,2048]{2,0,1:T(8,128)(2,1)} async-done(((bf16[128,8,2048]{2,0,1:T(8,128)(2,1)}), bf16[128,8,2048]{2,0,1:T(8,128)(2,1)}, u32[]{:S(2)}, u32[]{:S(2)}) %all-to-all-start) | async-done | bytes 4194336 | tf_op jit(solution)/shard_map/all_to_all | solution.py:47
  74.9 4.7 %all-to-all-start.1 = ((bf16[128,8,2048]{2,0,1:T(8,128)(2,1)}), bf16[128,8,2048]{2,0,1:T(8,128)(2,1)}, u32[]{:S(2)}, u32[]{:S(2)}) async-start(bf16[128,8,2048]{2,0,1:T(8,128)(2,1)} %bitcast.69), calls=%async_computation.1 | async-start | bytes 8388608 | tf_op jit(solution)/shard_map/all_to_all | solution.py:48
  79.6 0.0 all-gather.5.cloned.1.call-start
  79.7 0.0 copy-done.3
  79.7 0.3 convolution_convert_fusion
  80.0 0.9 copy.52
  80.9 0.0 all-gather.5.cloned.1.call-update
  80.9 0.6 reduce_sum.37
  82.2 3.6 %copy.67 = bf16[128,8,16,128]{3,2,1,0:T(8,128)(2,1)S(1)} copy(bf16[128,8,16,128]{3,1,2,0:T(8,128)(2,1)} %bitcast.30) | data formatting | bytes 8388608
  85.8 0.0 copy-done
  85.8 5.9 %multiply_convert_fusion.1 = (bf16[16,128,1024]{2,1,0:T(8,128)(2,1)}, bf16[16,128,1024]{2,1,0:T(8,128)(2,1)}) fusion(bf16[16,128,128]{2,1,0:T(8,128)(2,1)S(1)} %bitcast.63, bf16[1024,16,128]{2,1,0:T(8,128)(2,1)S(1)} %bitcast.65), kind=kOutput, calls=%fused_computation.4 | convolution fusion | flops 545259520 | bytes 13107200 | tf_op jit(solution)/shard_map/nbk,bkc->nbc/dot_general | solution.py:18
  91.8 7.8 %convert_element_type.86 = bf16[4,256,2048]{1,0,2:T(4,128)(2,1)} reshape(bf16[1024,16,128]{0,2,1:T(8,128)(2,1)} %bitcast.66) | data formatting | bytes 8388608 | tf_op jit(solution)/shard_map/convert_element_type | solution.py:50
  99.6 37.5 %all-to-all-done.1 = bf16[128,8,2048]{2,0,1:T(8,128)(2,1)} async-done(((bf16[128,8,2048]{2,0,1:T(8,128)(2,1)}), bf16[128,8,2048]{2,0,1:T(8,128)(2,1)}, u32[]{:S(2)}, u32[]{:S(2)}) %all-to-all-start.1) | async-done | bytes 4194336 | tf_op jit(solution)/shard_map/all_to_all | solution.py:48
  137.1 3.6 %copy.68 = bf16[128,8,16,128]{3,2,1,0:T(8,128)(2,1)S(1)} copy(bf16[128,8,16,128]{3,1,2,0:T(8,128)(2,1)} %bitcast.34) | data formatting | bytes 8388608
  140.7 5.8 %convert_convert_fusion = f32[16,128,1024]{2,1,0:T(8,128)} fusion(bf16[16,128,128]{2,1,0:T(8,128)(2,1)S(1)} %bitcast.64, bf16[1024,16,128]{2,1,0:T(8,128)(2,1)S(1)} %bitcast.67), kind=kOutput, calls=%fused_computation.12 | convolution fusion | flops 541065216 | bytes 13107200 | tf_op jit(solution)/shard_map/nbk,bkc->nbc/dot_general | solution.py:18
  146.5 13.9 %add_divide_fusion = (f32[1024,2048]{1,0:T(8,128)}, f32[1024,2048]{1,0:T(8,128)}) fusion(f32[]{:T(128)S(6)} %convert_element_type.84, bf16[1024,2048]{0,1:T(8,128)(2,1)} %bitcast.71, bf16[1024,1024]{1,0:T(8,128)(2,1)} %all-gather.3.cloned.1.call-done), kind=kOutput, calls=%fused_computation.3 | convolution fusion | flops 4304404480 | bytes 23068676 | tf_op jit(solution)/shard_map/ti,tj->ij/dot_general | solution.py:56
  160.4 30.5 %fusion = f32[4,1024]{1,0:T(4,128)S(1)} fusion(f32[1024,2048]{0,1:T(8,128)} %bitcast.70, bf16[4,256,1024]{2,1,0:T(8,128)(2,1)S(1)} %bitcast.78, f32[4]{0:T(128)S(1)} %convert_rsqrt_fusion, f32[1024,2048]{1,0:T(8,128)} %get-tuple-element.4, bf16[4,256,2048]{1,0,2:T(4,128)(2,1)} %convert_element_type.86, bf16[1024,1024]{1,0:T(8,128)(2,1)} %all-gather.5.cloned.1.call-done), kind=kOutput, calls=%fused_computation.1 | convolution fusion | flops 21516775424 | bytes 25182224 | tf_op jit(solution)/shard_map/ui,sij->suj/dot_general | solution.py:67
  191.0 0.1 reshape.108
  191.1 0.1 reduce_sum.39
  191.2 40.3 %psum.7 = f32[64,4]{0,1:T(4,128)} all-reduce(f32[64,4]{0,1:T(4,128)S(1)} %multiply_bitcast_fusion), channel_id=1, replica_groups=mesh['dp'=8,'mp'=4] {'dp','mp'}, use_global_device_ids=true, to_apply=%region_4.5 | all-reduce | flops 256 | bytes 2048 | tf_op jit(solution)/shard_map/psum | solution.py:71
  231.5 0.0 copy-done.1
  (15 shorter events, 0.1 us)
Async XLA Ops:
  7.2 78.6 %copy-start = (bf16[2048,128]{1,0:T(8,128)(2,1)S(1)}, bf16[2048,128]{1,0:T(8,128)(2,1)}, u32[]{:S(2)}) copy-start(bf16[2048,128]{1,0:T(8,128)(2,1)} %param.12) | copy-start | bytes 1572868
  12.0 5.4 %copy-start.2 = (bf16[1024,128]{1,0:T(8,128)(2,1)S(1)}, bf16[1024,128]{1,0:T(8,128)(2,1)}, u32[]{:S(2)}) copy-start(bf16[1024,128]{1,0:T(8,128)(2,1)} %param.11) | copy-start | bytes 786436
  12.0 5.4 %copy-start.4 = (bf16[128,1024]{1,0:T(8,128)(2,1)S(1)}, bf16[128,1024]{1,0:T(8,128)(2,1)}, u32[]{:S(2)}) copy-start(bf16[128,1024]{1,0:T(8,128)(2,1)} %param.7) | copy-start | bytes 786436
  12.0 6.0 %copy-start.6 = (s32[4]{0:T(128)S(1)}, s32[4]{0:T(128)}, u32[]{:S(2)}) copy-start(s32[4]{0:T(128)} %param.13) | copy-start | bytes 52
  12.0 62.9 %all-to-all-start = ((bf16[128,8,2048]{2,0,1:T(8,128)(2,1)}), bf16[128,8,2048]{2,0,1:T(8,128)(2,1)}, u32[]{:S(2)}, u32[]{:S(2)}) async-start(bf16[128,8,2048]{2,0,1:T(8,128)(2,1)} %bitcast.68), calls=%async_computation | async-start | bytes 8388608 | tf_op jit(solution)/shard_map/all_to_all | solution.py:47
  17.4 129.2 %all-gather.3.cloned.1.call-start = ((), (), s32[]{:S(2)}) async-start(), calls=%async_computation.2 | async-start | bytes 2359296 | tf_op jit(solution)/shard_map/all_gather | solution.py:43
  74.9 4.8 %copy-start.3 = (bf16[128,1024]{1,0:T(8,128)(2,1)S(1)}, bf16[128,1024]{1,0:T(8,128)(2,1)}, u32[]{:S(2)}) copy-start(bf16[128,1024]{1,0:T(8,128)(2,1)} %param.9) | copy-start | bytes 786436
  74.9 62.2 %all-to-all-start.1 = ((bf16[128,8,2048]{2,0,1:T(8,128)(2,1)}), bf16[128,8,2048]{2,0,1:T(8,128)(2,1)}, u32[]{:S(2)}, u32[]{:S(2)}) async-start(bf16[128,8,2048]{2,0,1:T(8,128)(2,1)} %bitcast.69), calls=%async_computation.1 | async-start | bytes 8388608 | tf_op jit(solution)/shard_map/all_to_all | solution.py:48
  79.6 80.8 %all-gather.5.cloned.1.call-start = ((), (), s32[]{:S(2)}) async-start(), calls=%async_computation.3 | async-start | bytes 2359296 | tf_op jit(solution)/shard_map/all_gather | solution.py:44
  146.5 13.9 %copy-start.5 = (bf16[1024,1024]{1,0:T(8,128)(2,1)S(1)}, bf16[1024,1024]{1,0:T(8,128)(2,1)}, u32[]{:S(2)}) copy-start(bf16[1024,1024]{1,0:T(8,128)(2,1)} %all-gather.3.cloned.1.call-done) | copy-start | bytes 6291460
  160.4 71.1 %copy-start.1 = (bf16[2048,128]{1,0:T(8,128)(2,1)S(1)}, bf16[2048,128]{1,0:T(8,128)(2,1)}, u32[]{:S(2)}) copy-start(bf16[2048,128]{1,0:T(8,128)(2,1)} %param.12) | copy-start | bytes 1572868
Sparse Core Ops, SparseCore 0:
  20.1 49.0 all-gather.2
  82.4 48.9 all-gather.4
where the time goes:
time: 239 us; the launch traced here: 238 us
  waiting for transfers between devices  88.8 us (37%)
  matrix products  56.8 us (24%)
  blocking collectives  40.3 us (17%)
  local copies, waits for them, and re-layouts  25.7 us (11%)
  between operations  14.8 us (6%)
  starting transfers between devices  10.1 us (4%)
    all_to_all x1, waiting for transfers between devices, local(): lax.all_to_all(grad_in, 'dp', split_axis=1, concat_axis=0, tiled=True)  51.3 us
    psum x1, blocking collectives, local(): scores = lax.psum(partial_scores, ('dp', 'mp'))  40.3 us
    all_to_all x1, waiting for transfers between devices, local(): lax.all_to_all(query_grad, 'dp', split_axis=1, concat_axis=0, tiled=True)  37.5 us
    dot_general x1, matrix products, local(): jnp.einsum('ui,sij->suj', gathered_query, precond, preferred_element_type...  30.5 us
    dot_general x1, matrix products, local(): jnp.einsum('ti,tj->ij', act_square, grad_square, preferred_element_type=j...  13.9 us
    dot_general x4, matrix products, rotate(): jnp.einsum('nbk,bkc->nbc', rows_in.reshape(count_rows, blocks, block_size...  12.4 us
    convert_element_type x1, local copies, waits for them, and re-layouts, local(): grad_rot = rotate(grad_cols, grad_basis).astype(jnp.bfloat16)  7.83 us
    unnamed x16, local copies, waits for them, and re-layouts  7.19 us
  transfers between devices with their start and end apart: 4, of which 2 were waited for; matrix products, arithmetic and copies ran while one was open for 20% of the time, Pallas kernels for 0%

commit v1 on v0

--- a/solution.py
+++ b/solution.py
@@ -45,7 +45,12 @@
     )
     grad_cols, query_cols = (
         lax.all_to_all(grad_in, "dp", split_axis=1, concat_axis=0, tiled=True),
-        lax.all_to_all(query_grad, "dp", split_axis=1, concat_axis=0, tiled=True),
+        jnp.concatenate(
+            lax.all_to_all(
+                jnp.stack(jnp.split(query_grad, lax.axis_size("dp"), axis=1)), "dp", 0, 0
+            ),
+            axis=0,
+        ),
     )
     grad_rot = rotate(grad_cols, grad_basis).astype(jnp.bfloat16)
     query_grad_rot = rotate(query_cols, grad_basis).astype(jnp.bfloat16)

time: 239 us -> 241 us (level)
  local copies, waits for them, and re-layouts: 25.7 us -> 36.1 us
  waiting for transfers between devices: 88.8 us -> 79.8 us
    unnamed x16 -> x21, local copies, waits for them, and re-layouts: 7.19 us -> 20.4 us
    all_to_all x1, waiting for transfers between devices: 51.3 us -> 42.2 us  [local(): lax.all_to_all(grad_in, 'dp', split_axis=1, concat_axis=0, tiled=True)]
    all_to_all x1 -> x0, local copies, waits for them, and re-layouts: 4.72 us -> none  [local(): lax.all_to_all(query_grad, 'dp', split_axis=1, concat_axis=0, tiled=True)]
  transfers between devices with their start and end apart: 4 -> 4, of which waited for: 2 -> 2; matrix products, arithmetic and copies ran while one was open for 20% -> 26% of each run, Pallas kernels for 0% -> 0%
where the time goes in v1:
time: 241 us; the launch traced here: 240 us
  waiting for transfers between devices  79.8 us (33%)
  matrix products  58 us (24%)
  blocking collectives  39.3 us (16%)
  local copies, waits for them, and re-layouts  36.1 us (15%)
  between operations  14.8 us (6%)
  starting transfers between devices  9.84 us (4%)
    all_to_all x1, waiting for transfers between devices, local(): lax.all_to_all(grad_in, 'dp', split_axis=1, concat_axis=0, tiled=True)  42.2 us
    psum x1, blocking collectives, local(): scores = lax.psum(partial_scores, ('dp', 'mp'))  39.3 us
    all_to_all x1, waiting for transfers between devices, local(): lax.all_to_all(jnp.stack(jnp.split(query_grad, lax.axis_size('dp'), axis=...  37.5 us
    dot_general x1, matrix products, local(): jnp.einsum('ui,sij->suj', gathered_query, precond, preferred_element_type...  30.5 us
    unnamed x21, local copies, waits for them, and re-layouts  20.4 us
    dot_general x1, matrix products, local(): jnp.einsum('ti,tj->ij', act_square, grad_square, preferred_element_type=j...  13.9 us
    dot_general x4, matrix products, rotate(): jnp.einsum('nbk,bkc->nbc', rows_in.reshape(count_rows, blocks, block_size...  13.6 us
    convert_element_type x1, local copies, waits for them, and re-layouts, local(): grad_rot = rotate(grad_cols, grad_basis).astype(jnp.bfloat16)  7.82 us
  transfers between devices with their start and end apart: 4, of which 2 were waited for; matrix products, arithmetic and copies ran while one was open for 26% of the time, Pallas kernels for 0%

profile of v1, /device:TPU:0, one launch (start us, length us, event | category | flops | bytes accessed | tf_op | source)
XLA Modules:
  0.0 240.2 jit_solution(787329138706612825)
XLA Ops:
  7.2 0.0 all-gather.3.cloned.1.call-start
  7.2 0.8 select_reduce_fusion
  8.0 1.4 fusion.15
  9.4 0.2 copy.42
  9.6 0.8 multiply_convert_fusion.4
  10.4 4.8 %copy.87 = bf16[16,8,8,2048]{3,2,0,1:T(8,128)(2,1)} copy(bf16[16,8,8,2048]{3,2,1,0:T(8,128)(2,1)} %bitcast.82) | data formatting | bytes 8388608 | tf_op jit(solution)/shard_map/all_to_all | solution.py:47
  15.2 5.2 %all-to-all-start = ((bf16[128,8,2048]{2,0,1:T(8,128)(2,1)}), bf16[128,8,2048]{2,0,1:T(8,128)(2,1)}, u32[]{:S(2)}, u32[]{:S(2)}) async-start(bf16[128,8,2048]{2,0,1:T(8,128)(2,1)} %bitcast.79), calls=%async_computation | async-start | bytes 8388608 | tf_op jit(solution)/shard_map/all_to_all | solution.py:47
  20.4 1.9 bitcast_dynamic-update-slice_fusion.7
  22.4 1.9 bitcast_dynamic-update-slice_fusion.6
  24.3 1.9 bitcast_dynamic-update-slice_fusion.5
  26.2 1.9 bitcast_dynamic-update-slice_fusion.4
  28.0 1.9 bitcast_dynamic-update-slice_fusion.3
  29.9 1.9 bitcast_dynamic-update-slice_fusion.2
  31.8 1.9 bitcast_dynamic-update-slice_fusion.1
  33.7 1.9 bitcast_dynamic-update-slice_fusion
  35.6 42.2 %all-to-all-done = bf16[128,8,2048]{2,0,1:T(8,128)(2,1)} async-done(((bf16[128,8,2048]{2,0,1:T(8,128)(2,1)}), bf16[128,8,2048]{2,0,1:T(8,128)(2,1)}, u32[]{:S(2)}, u32[]{:S(2)}) %all-to-all-start) | async-done | bytes 4194336 | tf_op jit(solution)/shard_map/all_to_all | solution.py:47
  77.8 4.6 %all-to-all-start.1 = ((bf16[8,128,2048]{2,1,0:T(8,128)(2,1)}), bf16[8,128,2048]{2,1,0:T(8,128)(2,1)}, u32[]{:S(2)}, u32[]{:S(2)}) async-start(bf16[8,128,2048]{2,1,0:T(8,128)(2,1)} %bitcast_dynamic-update-slice_fusion), calls=%async_computation.1 | async-start | bytes 8388608 | tf_op jit(solution)/shard_map/all_to_all | solution.py:49
  82.4 0.0 all-gather.5.cloned.1.call-start
  82.4 0.3 convolution_convert_fusion
  82.8 0.9 copy.50
  83.7 0.6 reduce_sum.37
  85.0 3.6 %copy.63 = bf16[128,8,16,128]{3,2,1,0:T(8,128)(2,1)S(1)} copy(bf16[128,8,16,128]{3,1,2,0:T(8,128)(2,1)} %bitcast.35) | data formatting | bytes 8388608
  88.5 5.9 %multiply_convert_fusion.1 = (bf16[16,128,1024]{2,1,0:T(8,128)(2,1)}, bf16[16,128,1024]{2,1,0:T(8,128)(2,1)}) fusion(bf16[16,128,128]{2,1,0:T(8,128)(2,1)S(1)} %bitcast.74, bf16[1024,16,128]{2,1,0:T(8,128)(2,1)S(1)} %bitcast.76), kind=kOutput, calls=%fused_computation.4 | convolution fusion | flops 545259520 | bytes 13107200 | tf_op jit(solution)/shard_map/nbk,bkc->nbc/dot_general | solution.py:18
  94.5 7.8 %convert_element_type.86 = bf16[4,256,2048]{1,0,2:T(4,128)(2,1)} reshape(bf16[1024,16,128]{0,2,1:T(8,128)(2,1)} %bitcast.77) | data formatting | bytes 8388608 | tf_op jit(solution)/shard_map/convert_element_type | solution.py:55
  102.3 37.5 %all-to-all-done.1 = bf16[8,128,2048]{2,1,0:T(8,128)(2,1)} async-done(((bf16[8,128,2048]{2,1,0:T(8,128)(2,1)}), bf16[8,128,2048]{2,1,0:T(8,128)(2,1)}, u32[]{:S(2)}, u32[]{:S(2)}) %all-to-all-start.1) | async-done | bytes 4194336 | tf_op jit(solution)/shard_map/all_to_all | solution.py:49
  139.8 3.6 %copy.64 = bf16[128,8,16,128]{3,2,1,0:T(8,128)(2,1)S(1)} copy(bf16[128,8,16,128]{3,1,2,0:T(8,128)(2,1)} %bitcast.39) | data formatting | bytes 8388608
  143.4 5.9 %convert_convert_fusion = f32[16,1024,128]{1,2,0:T(8,128)} fusion(bf16[16,128,128]{2,1,0:T(8,128)(2,1)S(1)} %bitcast.75, bf16[1024,16,128]{2,1,0:T(8,128)(2,1)S(1)} %bitcast.78), kind=kOutput, calls=%fused_computation.11 | convolution fusion | flops 541065216 | bytes 13107200 | tf_op jit(solution)/shard_map/nbk,bkc->nbc/dot_general | solution.py:18
  149.4 13.9 %add_divide_fusion = (f32[1024,2048]{1,0:T(8,128)}, f32[1024,2048]{1,0:T(8,128)}) fusion(f32[]{:T(128)S(6)} %convert_element_type.84, bf16[1024,2048]{0,1:T(8,128)(2,1)} %bitcast.81, bf16[1024,1024]{1,0:T(8,128)(2,1)} %all-gather.3.cloned.1.call-done), kind=kOutput, calls=%fused_computation.3 | convolution fusion | flops 4304404480 | bytes 23068676 | tf_op jit(solution)/shard_map/ti,tj->ij/dot_general | solution.py:61
  163.3 30.5 %fusion = f32[4,1024]{1,0:T(4,128)S(1)} fusion(f32[1024,2048]{0,1:T(8,128)} %bitcast.80, bf16[4,256,1024]{2,1,0:T(8,128)(2,1)S(1)} %bitcast.87, f32[4]{0:T(128)S(1)} %convert_rsqrt_fusion, f32[1024,2048]{1,0:T(8,128)} %get-tuple-element.4, bf16[4,256,2048]{1,0,2:T(4,128)(2,1)} %convert_element_type.86, bf16[1024,1024]{1,0:T(8,128)(2,1)} %all-gather.5.cloned.1.call-done), kind=kOutput, calls=%fused_computation.1 | convolution fusion | flops 21516775424 | bytes 25182224 | tf_op jit(solution)/shard_map/ui,sij->suj/dot_general | solution.py:72
  193.8 0.1 reshape.100
  193.9 0.1 reduce_sum.39
  194.1 39.3 %psum.7 = f32[64,4]{0,1:T(4,128)} all-reduce(f32[64,4]{0,1:T(4,128)S(1)} %multiply_bitcast_fusion), channel_id=1, replica_groups=mesh['dp'=8,'mp'=4] {'dp','mp'}, use_global_device_ids=true, to_apply=%region_4.5 | all-reduce | flops 256 | bytes 2048 | tf_op jit(solution)/shard_map/psum | solution.py:76
  (20 shorter events, 0.1 us)
Async XLA Ops:
  7.2 81.4 %copy-start = (bf16[2048,128]{1,0:T(8,128)(2,1)S(1)}, bf16[2048,128]{1,0:T(8,128)(2,1)}, u32[]{:S(2)}) copy-start(bf16[2048,128]{1,0:T(8,128)(2,1)} %param.12) | copy-start | bytes 1572868
  7.2 142.2 %all-gather.3.cloned.1.call-start = ((), (), s32[]{:S(2)}) async-start(), calls=%async_computation.2 | async-start | bytes 2359296 | tf_op jit(solution)/shard_map/all_gather | solution.py:43
  15.2 62.6 %all-to-all-start = ((bf16[128,8,2048]{2,0,1:T(8,128)(2,1)}), bf16[128,8,2048]{2,0,1:T(8,128)(2,1)}, u32[]{:S(2)}, u32[]{:S(2)}) async-start(bf16[128,8,2048]{2,0,1:T(8,128)(2,1)} %bitcast.79), calls=%async_computation | async-start | bytes 8388608 | tf_op jit(solution)/shard_map/all_to_all | solution.py:47
  35.6 46.9 %copy-start.2 = (bf16[1024,128]{1,0:T(8,128)(2,1)S(1)}, bf16[1024,128]{1,0:T(8,128)(2,1)}, u32[]{:S(2)}) copy-start(bf16[1024,128]{1,0:T(8,128)(2,1)} %param.11) | copy-start | bytes 786436
  35.6 46.9 %copy-start.3 = (bf16[128,1024]{1,0:T(8,128)(2,1)S(1)}, bf16[128,1024]{1,0:T(8,128)(2,1)}, u32[]{:S(2)}) copy-start(bf16[128,1024]{1,0:T(8,128)(2,1)} %param.9) | copy-start | bytes 786436
  35.6 48.1 %copy-start.5 = (s32[4]{0:T(128)S(1)}, s32[4]{0:T(128)}, u32[]{:S(2)}) copy-start(s32[4]{0:T(128)} %param.13) | copy-start | bytes 52
  77.8 62.0 %all-to-all-start.1 = ((bf16[8,128,2048]{2,1,0:T(8,128)(2,1)}), bf16[8,128,2048]{2,1,0:T(8,128)(2,1)}, u32[]{:S(2)}, u32[]{:S(2)}) async-start(bf16[8,128,2048]{2,1,0:T(8,128)(2,1)} %bitcast_dynamic-update-slice_fusion), calls=%async_computation.1 | async-start | bytes 8388608 | tf_op jit(solution)/shard_map/all_to_all | solution.py:49
  82.4 80.9 %all-gather.5.cloned.1.call-start = ((), (), s32[]{:S(2)}) async-start(), calls=%async_computation.3 | async-start | bytes 2359296 | tf_op jit(solution)/shard_map/all_gather | solution.py:44
  149.4 13.9 %copy-start.4 = (bf16[1024,1024]{1,0:T(8,128)(2,1)S(1)}, bf16[1024,1024]{1,0:T(8,128)(2,1)}, u32[]{:S(2)}) copy-start(bf16[1024,1024]{1,0:T(8,128)(2,1)} %all-gather.3.cloned.1.call-done) | copy-start | bytes 6291460
  163.3 70.1 %copy-start.1 = (bf16[2048,128]{1,0:T(8,128)(2,1)S(1)}, bf16[2048,128]{1,0:T(8,128)(2,1)}, u32[]{:S(2)}) copy-start(bf16[2048,128]{1,0:T(8,128)(2,1)} %param.12) | copy-start | bytes 1572868
Sparse Core Ops, SparseCore 0:
  10.6 51.8 all-gather.2
  85.1 47.9 all-gather.4
